TPU v7x, 256 devices: a whole 4x4x8 slice. The times are simulated.
256 devices in a mesh: grp: 8 (over x, core), tok: 32 (over y, z).
Axes of the slice: x: 4, y: 4, z: 8, core: 2. Of those that a mesh axis runs over, the one named last changes fastest.
Arguments:
- hidden_in: bfloat16 [12288, 2048], P('tok', 'grp'), may hold values from -6 to 6
- w_qkv: float32 [2048, 6144], P(('grp', 'tok')), may hold values from -1 to 1
- w_out: float32 [2048, 2048], P(('grp', 'tok')), may hold values from -0.125 to 0.125
- qkv_bias: float32 [6144], P('grp'), may hold values from -3 to 3
- out_bias: float32 [2048], P('grp'), may hold values from -3 to 3
- ln_gain: float32 [2048], replicated, may hold values from 0.5 to 1.5
- ln_bias: float32 [2048], replicated, may hold values from -2 to 2
- cache_k: bfloat16 [8192, 2048], P('tok', 'grp'), may hold values from -300 to 300
- cache_v: bfloat16 [8192, 2048], P('tok', 'grp'), may hold values from -6 to 6
- prompt_lengths: int32 [8], replicated, may hold values from 1 to 9216, 12288 in all
- cache_lengths: int32 [8], replicated, may hold values from 0 to 256, as said below
- cache_holders: int32 [8], replicated, may hold values from 0 to 31, as said below
Outputs:
- layer_out: bfloat16 [12288, 2048], P('tok', 'grp')
Inputs may be any that keep to these rules, and one draw needn't show every extreme that they name: `prompt_lengths`: the lengths sum to 12288 and the longest is exactly 9216. `cache_lengths`: 4 prompts have a cache of 1 to 256 positions and the others none; some prompt has exactly 256. `cache_holders`: the 8 holders are distinct.
All inputs are finite; a program needn't handle non-finite values.
Results may differ from a plain program's by a relative error of at most 0.013.
Values may be sent and summed in bfloat16 or wider, within the bound.
No kernel may reach another device: no remote copies, remote signals or barrier semaphores. Data moves between devices by JAX's collectives and lax.ppermute only.
A program may use at most 128 MiB of HBM per device.

v0:
```python
import math

import jax
import jax.numpy as jnp
from jax import lax
from jax.experimental import pallas as pl
from jax.experimental.pallas import tpu as pltpu
from jax.sharding import Mesh, PartitionSpec as P

HD = 256
ROT = 64
P_SIZE = 8
NX, NC, NY, NZ = 4, 2, 4, 8
SIZES = {"x": NX, "c": NC, "y": NY, "z": NZ}
NEG = -1e30
SCALE2 = math.log2(math.e) / math.sqrt(HD)
BF = jnp.bfloat16
F32 = jnp.float32


def shift(value, axis, by):
    n = SIZES[axis]
    return lax.ppermute(value, axis, [(i, (i + by) % n) for i in range(n)])


RING4 = (0, -1, 1, 2)
RING8 = (0, -1, 1, -2, 2, -3, 3, 4)


def vmem():
    return pl.BlockSpec(memory_space=pltpu.VMEM)


def smem():
    return pl.BlockSpec(memory_space=pltpu.SMEM)


def hbm():
    return pl.BlockSpec(memory_space=pltpu.HBM)


def params(mb=16):
    return pltpu.CompilerParams(vmem_limit_bytes=mb << 20)


def norm_kernel(whole, gain, bias, out):
    groups, rows, _ = whole.shape
    total = jnp.zeros((rows, 1), F32)
    for g in range(groups):
        total += jnp.sum(whole[g].astype(F32), axis=1, keepdims=True)
    mean = total * (1.0 / (groups * HD))
    square = jnp.zeros((rows, 1), F32)
    for g in range(groups):
        d = whole[g].astype(F32) - mean
        square += jnp.sum(d * d, axis=1, keepdims=True)
    scale = lax.rsqrt(square * (1.0 / (groups * HD)) + 1e-05)
    for g in range(groups):
        d = whole[g].astype(F32) - mean
        out[g] = (d * scale * gain[g] + bias[g]).astype(BF)


def norm_call(whole, gain, bias):
    return pl.pallas_call(
        norm_kernel,
        out_shape=jax.ShapeDtypeStruct(whole.shape, BF),
        in_specs=[vmem()] * 3,
        out_specs=vmem(),
        compiler_params=params(),
        name="norm",
    )(whole, gain, bias)


def prep_kernel(a, b, out):
    for g in range(NX * NC):
        out[g, :, : 3 * HD] = a[:, g * 3 * HD : (g + 1) * 3 * HD].astype(BF)
        out[g, :, 3 * HD :] = b[:, g * HD : (g + 1) * HD].astype(BF)


def prep_call(a, b):
    return pl.pallas_call(
        prep_kernel,
        out_shape=jax.ShapeDtypeStruct((NX * NC, 8, 4 * HD), BF),
        in_specs=[vmem(), vmem()],
        out_specs=vmem(),
        compiler_params=params(8),
        name="prep",
    )(a, b)


def proj_kernel(pos, normed, bias, cosw, sinl, sinr, *refs):
    blocks, (q_out, kv_out, wbuf, sem) = refs[:8], refs[8:]
    copies = []
    for n, ref in enumerate(blocks):
        row = lax.rem(pos[2] + RING4[n // 2] + NY, NY) * NZ
        for i in range(NZ // 2):
            at = row + lax.rem(pos[3] + RING8[(n % 2) * (NZ // 2) + i] + NZ, NZ)
            copies.append(pltpu.make_async_copy(ref.at[i], wbuf.at[:, at], sem.at[len(copies)]))
    for c in copies:
        c.start()
    for c in copies:
        c.wait()
    rows = normed.shape[1]

    def part(n):
        total = jnp.broadcast_to(bias[:, n * HD : (n + 1) * HD], (rows, HD))
        for g in range(NX * NC):
            w = wbuf[g, :, :, n * HD : (n + 1) * HD].reshape(NY * NZ * 8, HD)
            total += jnp.dot(normed[g], w, preferred_element_type=F32)
        return total

    def rotated(value):
        head = value[:, :128]
        back = pltpu.roll(head, 128 - ROT // 2, 1)
        fwd = pltpu.roll(head, ROT // 2, 1)
        return head * cosw[...] + back * sinl[...] + fwd * sinr[...]

    q = part(0)
    head, tail = rotated(q).astype(BF), q[:, 128:].astype(BF)
    for i in range(NY):
        q_out[i, :, :128] = head
        q_out[i, :, 128:] = tail
    k = part(1)
    kv_out[:rows, :128] = rotated(k).astype(BF)
    kv_out[:rows, 128:] = k[:, 128:].astype(BF)
    kv_out[rows:] = part(2).astype(BF)


def proj_call(pos, normed, bias, tables, blocks):
    rows = normed.shape[1]
    return pl.pallas_call(
        proj_kernel,
        out_shape=(
            jax.ShapeDtypeStruct((NY, rows, HD), BF),
            jax.ShapeDtypeStruct((2 * rows, HD), BF),
        ),
        in_specs=[smem()] + [vmem()] * 5 + [hbm()] * 8,
        out_specs=(vmem(), vmem()),
        scratch_shapes=[
            pltpu.VMEM((NX * NC, NY * NZ, 8, 3 * HD), BF),
            pltpu.SemaphoreType.DMA((NY * NZ,)),
        ],
        compiler_params=params(24),
        name="proj",
    )(pos, normed, bias, *tables, *blocks)


def attend_call(pos, plen, clen, hold, q, blocks, shifts, cache=None, state=None, last=False):
    rows = q.shape[1]
    flat, where = [], []
    for b in blocks:
        if isinstance(b, tuple):
            where.append((len(flat), 0, len(flat) + 1, 0))
            flat += list(b)
        else:
            where.append((len(flat), 0, len(flat), rows))
            flat.append(b)

    def kernel(pos, plen, clen, hold, q, *refs):
        refs = list(refs)
        kv = [refs.pop(0) for _ in flat]
        cb = refs.pop(0) if cache is not None else None
        old = (refs.pop(0), refs.pop(0)) if state is not None else None
        cbuf, csem = (refs.pop(), refs.pop())[::-1] if cache is not None else (None, None)
        if last:
            out, acc, stat, vt = refs
        else:
            acc, stat, vt = refs
        starts, ends = [], []
        run = jnp.int32(0)
        for p in range(P_SIZE):
            starts.append(run)
            run = run + plen[p]
            ends.append(run)
        if old is None:
            acc[...] = jnp.zeros_like(acc)
            stat[:, 0:1] = jnp.full((NY, 1, rows), NEG, F32)
            stat[:, 1:2] = jnp.zeros((NY, 1, rows), F32)
        else:
            acc[...] = old[0][...]
            stat[...] = old[1][...]
        lane = lax.broadcasted_iota(jnp.int32, (1, rows), 1)

        def limits(j):
            first = (j * NZ + pos[3]) * rows
            n = first + lane
            qs = jnp.zeros((1, rows), jnp.int32)
            qs_first = jnp.int32(0)
            for p in range(1, P_SIZE):
                qs = jnp.where(n >= starts[p], starts[p], qs)
                qs_first = jnp.where(first >= starts[p], starts[p], qs_first)
            return first, n, qs, qs_first

        def fold(j, k, count, low, high):
            index = lax.broadcasted_iota(jnp.int32, (count, rows), 0)
            for cut in (slice(0, rows),):
                s = lax.dot_general(k, q[j, cut], (((1,), (1,)), ((), ())), preferred_element_type=F32)
                s = jnp.where((index >= low[:, cut]) & (index <= high[:, cut]), s, NEG)
                m_old = stat[j, 0:1, cut]
                m_new = jnp.maximum(m_old, jnp.max(s, axis=0, keepdims=True))
                w = jnp.exp2((s - m_new) * SCALE2)
                alpha = jnp.exp2((m_old - m_new) * SCALE2)
                stat[j, 0:1, cut] = m_new
                stat[j, 1:2, cut] = stat[j, 1:2, cut] * alpha + jnp.sum(w, axis=0, keepdims=True)
                acc[j, :, cut] = acc[j, :, cut] * alpha + jnp.dot(
                    vt[:, :count], w.astype(BF), preferred_element_type=F32
                )

        for (ki, ko, vi, vo), by in zip(where, shifts):
            tk = pos[2] * NZ + lax.rem(pos[3] + by + NZ, NZ)
            base = tk * rows
            vt[...] = jnp.transpose(kv[vi][vo : vo + rows].astype(F32)).astype(BF)

            def one_query(j, carry):
                first, n, qs, qs_first = limits(j)

                @pl.when((base <= first) & (base + rows - 1 >= qs_first))
                def _():
                    fold(j, kv[ki][ko : ko + rows], rows, qs - base, n - base)

                return carry

            lax.fori_loop(pos[2], NY, one_query, 0)

        if cb is not None:
            count = cbuf.shape[0] // 2

            def one_cache(b, carry):
                dev = pos[2] * NZ + b
                begin, end, length = jnp.int32(0), jnp.int32(0), jnp.int32(0)
                for p in range(P_SIZE):
                    hit = hold[p] == dev
                    begin = jnp.where(hit, starts[p], begin)
                    end = jnp.where(hit, ends[p], end)
                    length = jnp.where(hit, clen[p], length)

                @pl.when(length > 0)
                def _():
                    copy = pltpu.make_async_copy(cb.at[b, pl.ds(0, 2 * count)], cbuf, csem)
                    copy.start()
                    copy.wait()
                    vt[:, :count] = jnp.transpose(cbuf[count:].astype(F32)).astype(BF)

                    def one_query(j, carry2):
                        first, n, qs, qs_first = limits(j)

                        @pl.when((begin < first + rows) & (end > first))
                        def _():
                            ours = (n >= begin) & (n < end)
                            high = jnp.where(ours, length - 1, -1)
                            fold(j, cbuf[:count], count, jnp.zeros_like(high), high)

                        return carry2

                    lax.fori_loop(0, NY, one_query, 0)

                return carry

            lax.fori_loop(0, NZ, one_cache, 0)

        if last:

            def finish(j, carry):
                m = stat[j, 0:1]
                l = stat[j, 1:2]
                out[j, :HD] = (acc[j] * (1.0 / jnp.where(l > 0.0, l, 1.0))).astype(BF)
                parts = []
                for value in (m, l):
                    for _ in range(3):
                        piece = value.astype(BF).astype(F32)
                        parts.append(piece)
                        value = value - piece
                parts.append(jnp.zeros((10, rows), F32))
                out[j, HD:] = jnp.concatenate(parts, axis=0).astype(BF)
                return carry

            lax.fori_loop(0, NY, finish, 0)

    acc_type = jax.ShapeDtypeStruct((NY, HD, rows), F32)
    stat_type = jax.ShapeDtypeStruct((NY, 8, rows), F32)
    scratch = [pltpu.VMEM((HD, rows), BF)]
    if last:
        out_shape = jax.ShapeDtypeStruct((NY, HD + 16, rows), BF)
        scratch = [pltpu.VMEM(t.shape, F32) for t in (acc_type, stat_type)] + scratch
    else:
        out_shape = (acc_type, stat_type)
    if cache is not None:
        scratch += [pltpu.VMEM((512, HD), BF), pltpu.SemaphoreType.DMA]
    specs = [vmem()] * (1 + len(flat)) + ([hbm()] if cache is not None else []) + [vmem()] * (2 if state is not None else 0)
    ins = [q] + flat + ([cache] if cache is not None else []) + (list(state) if state is not None else [])
    alias = {} if last or state is None else {4 + len(ins) - 2: 0, 4 + len(ins) - 1: 1}
    work = len(blocks) * 2.5 * rows * rows * HD * 4
    return pl.pallas_call(
        kernel,
        out_shape=out_shape,
        in_specs=[smem()] * 4 + specs,
        out_specs=vmem() if last else (vmem(), vmem()),
        scratch_shapes=scratch,
        input_output_aliases=alias,
        compiler_params=params(24),
        name="attend",
    )(pos, plen, clen, hold, *ins)


def combine_kernel(a, b, c, d, out):
    ms, ls = [], []
    for ref in (a, b, c, d):
        tail = ref[HD:].astype(F32)
        ms.append(tail[0:1] + tail[1:2] + tail[2:3])
        ls.append(tail[3:4] + tail[4:5] + tail[5:6])
    top = jnp.maximum(jnp.maximum(ms[0], ms[1]), jnp.maximum(ms[2], ms[3]))
    ws = [l * jnp.exp2((m - top) * SCALE2) for m, l in zip(ms, ls)]
    inv = 1.0 / (ws[0] + ws[1] + ws[2] + ws[3])
    total = None
    for ref, w in zip((a, b, c, d), ws):
        term = ref[:HD].astype(F32) * (w * inv)
        total = term if total is None else total + term
    done = jnp.transpose(total).astype(BF)
    for i in range(NX):
        out[i] = done


def combine_call(pieces):
    rows = pieces[0].shape[1]
    return pl.pallas_call(
        combine_kernel,
        out_shape=jax.ShapeDtypeStruct((NX, rows, HD), BF),
        in_specs=[vmem()] * 4,
        out_specs=vmem(),
        compiler_params=params(),
        name="combine",
    )(*pieces)


def final_kernel(pos, mine, other, hidden, bias, w, out):
    total = hidden[...].astype(F32) + bias[...]
    for flip, ref in ((0, mine), (1, other)):
        for k in range(NX):
            g = k * NC + (pos[1] ^ flip)
            wg = w[:, :, g].reshape(NY * NZ * 8, HD)
            total += jnp.dot(ref[k], wg, preferred_element_type=F32)
    out[...] = total.astype(BF)


def final_call(pos, mine, other, hidden, bias, w):
    rows = hidden.shape[0]
    return pl.pallas_call(
        final_kernel,
        out_shape=jax.ShapeDtypeStruct((rows, HD), BF),
        in_specs=[smem()] + [vmem()] * 5,
        out_specs=vmem(),
        compiler_params=params(),
        name="final",
    )(pos, mine, other, hidden, bias, w)


def spread(block, axis):
    n = SIZES[axis]
    return lax.all_to_all(jnp.broadcast_to(block[None], (n,) + block.shape), axis, 0, 0, tiled=True)


def z_gather(block):
    half = block.shape[0] // 2
    parts = [block]
    right, left = block, block
    for _ in range(3):
        right, left = shift(right, "z", 1), shift(left, "z", -1)
        parts += [right, left]
    parts += [shift(right[:half], "z", 1), shift(left[half:], "z", -1)]
    shape = (NZ // 2,) + block.shape
    return jnp.concatenate(parts[:4], axis=0).reshape(shape), jnp.concatenate(parts[4:], axis=0).reshape(shape)


def token_tables(first, rows, plen, clen):
    n = first + jnp.arange(rows, dtype=jnp.int32)
    ends = jnp.cumsum(plen)
    starts = ends - plen
    prompt = jnp.sum((n[:, None] >= ends[None, :]).astype(jnp.int32), axis=1)
    onehot = prompt[:, None] == jnp.arange(P_SIZE, dtype=jnp.int32)[None, :]
    position = n + jnp.sum(jnp.where(onehot, (clen - starts)[None, :], 0), axis=1)
    half = ROT // 2
    lane = jnp.arange(128, dtype=jnp.int32)
    frequency = 10000.0 ** (-2.0 * (lane % half).astype(F32) / ROT)
    angles = position.astype(F32)[:, None] * frequency[None, :]
    cosine, sine = jnp.cos(angles), jnp.sin(angles)
    cosw = jnp.where(lane < ROT, cosine, 1.0)
    sinl = jnp.where(lane < half, -sine, 0.0)
    sinr = jnp.where((lane >= half) & (lane < ROT), sine, 0.0)
    return cosw, sinl, sinr


def shards(hidden, w_qkv, w_out, qkv_bias, out_bias, gain, lbias, cache_k, cache_v, plen, clen, hold):
    rows = hidden.shape[0]
    x, c, y, z = (lax.axis_index(a) for a in "xcyz")
    pos = jnp.stack([x, c, y, z]).astype(jnp.int32)

    wide = lax.all_to_all(prep_call(w_qkv, w_out), ("x", "c"), 0, 0, tiled=True)
    w_in, w_o = wide[:, :, : 3 * HD], wide[:, :, 3 * HD :].reshape(8 * NX * NC, HD)
    near, far = z_gather(w_in)
    near, far, w_o, cache_k, cache_v = lax.optimization_barrier((near, far, w_o, cache_k, cache_v))
    ups, downs = [shift(near, "y", 1)], [shift(near, "y", -1)]
    ups, downs = ups + [shift(far, "y", 1)], downs + [shift(far, "y", -1)]
    slots = cache_k.shape[0]
    table = lax.all_gather(jnp.concatenate([cache_k, cache_v, w_o], axis=0), "z", axis=0, tiled=False)
    whole = lax.all_gather(hidden, ("x", "c"), axis=0, tiled=False)
    normed = norm_call(whole, gain.reshape(8, 1, HD), lbias.reshape(8, 1, HD))
    tables = token_tables((y * NZ + z) * rows, rows, plen, clen)
    w_blocks = [near, far, ups[0], ups[1], downs[0], downs[1], shift(ups[0], "y", 1), shift(downs[1], "y", -1)]

    q4, kv = proj_call(pos, normed, qkv_bias.reshape(1, 3 * HD), tables, w_blocks)
    q = lax.all_to_all(q4, "y", 0, 0, tiled=True)
    q, table = lax.optimization_barrier((q, table))
    w_o = table[:, 2 * slots :].reshape(NZ, NX * NC, 8, HD)
    w_o = lax.all_gather(w_o, "y", axis=0, tiled=False)
    meta = (pos, plen, clen, hold, q)
    r1, l1 = shift(kv, "z", 1), shift(kv, "z", -1)
    r2, l2 = shift(r1, "z", 1), shift(l1, "z", -1)
    state = attend_call(*meta, [kv, r1, l1], (0, -1, 1))
    r2, l2, state = lax.optimization_barrier((r2, l2, state))
    r3, l3 = shift(r2, "z", 1), shift(l2, "z", -1)
    state = attend_call(*meta, [r2, l2], (-2, 2), state=state)
    r3, l3, state = lax.optimization_barrier((r3, l3, state))
    far = shift(r3, "z", 1)
    state = attend_call(*meta, [r3, l3], (-3, 3), cache=table, state=state)
    far, state, w_o = lax.optimization_barrier((far, state, w_o))
    o = attend_call(*meta, [far], (4,), state=state, last=True)
    rows_of = [lax.dynamic_index_in_dim(o, lax.rem(y + by + NY, NY), 0, keepdims=False) for by in RING4]
    back = [rows_of[0], shift(rows_of[1], "y", -1), shift(rows_of[2], "y", 1), shift(rows_of[3], "y", 2)]
    a_mine = lax.all_to_all(combine_call(back), "x", 0, 0, tiled=True)
    a_other = lax.ppermute(a_mine, "c", [(0, 1), (1, 0)])
    return final_call(pos, a_mine, a_other, hidden, out_bias.reshape(1, HD), w_o)


def solution(mesh):
    fine = Mesh(mesh.devices.reshape(NX, NC, NY, NZ), ("x", "c", "y", "z"))
    tok, grp = ("y", "z"), ("x", "c")
    placed = (
        P(tok, grp),
        P(grp + tok, None),
        P(grp + tok, None),
        P(grp),
        P(grp),
        P(),
        P(),
        P(tok, grp),
        P(tok, grp),
        P(),
        P(),
        P(),
    )
    return jax.shard_map(shards, mesh=fine, in_specs=placed, out_specs=P(tok, grp), check_vma=False)
```

profile of v0, /device:TPU:1, one launch (start us, length us, event | category | flops | bytes accessed | tf_op | source)
XLA Modules:
  0.0 162.1 jit_solution(5458203769988189011)
XLA Ops:
  9.1 11.0 %all_to_all.15 = bf16[8,8,1024]{2,1,0:T(8,128)(2,1)S(1)} all-to-all(bf16[8,8,1024]{2,1,0:T(8,128)(2,1)S(1)} %prep.1), channel_id=1, replica_groups=mesh['x'=4,'c'=2,'y'=4,'z'=8] {'x','c'}, dimensions={0} | all-to-all | bytes 262144 | tf_op jit(solution)/shard_map/all_to_all | solution.py:396
  21.9 4.0 %collective-permute-start.1 = (bf16[8,8,768]{2,1,0:T(8,128)(2,1)S(1)}, bf16[8,8,768]{2,1,0:T(8,128)(2,1)S(1)}, u32[]{:S(2)}, u32[]{:S(2)}) collective-permute-start(bf16[8,8,768]{2,1,0:T(8,128)(2,1)S(1)} %slice.20), channel_id=1, source_target_pairs={{0,7},{1,0},{2,1},{3,2},{4,3},{5,4},{6,5},{7,6},{8,15},{9,8},{10,9... | collective-permute-start | bytes 294920 | tf_op jit(solution)/shard_map/ppermute | solution.py:23
  27.8 2.8 %collective-permute-start.3 = (bf16[8,8,768]{2,1,0:T(8,128)(2,1)S(1)}, bf16[8,8,768]{2,1,0:T(8,128)(2,1)S(1)}, u32[]{:S(2)}, u32[]{:S(2)}) collective-permute-start(bf16[8,8,768]{2,1,0:T(8,128)(2,1)S(1)} %collective-permute-done.1), channel_id=1, source_target_pairs={{0,7},{1,0},{2,1},{3,2},{4,3},{5,4},{6,5},{7,6},{8,15},{9,8},{10,9... | collective-permute-start | bytes 294920 | tf_op jit(solution)/shard_map/ppermute | solution.py:23
  30.6 2.3 %collective-permute-done.2 = bf16[8,8,768]{2,1,0:T(8,128)(2,1)S(1)} collective-permute-done((bf16[8,8,768]{2,1,0:T(8,128)(2,1)S(1)}, bf16[8,8,768]{2,1,0:T(8,128)(2,1)S(1)}, u32[]{:S(2)}, u32[]{:S(2)}) %collective-permute-start.2) | collective-permute-done | bytes 98336 | tf_op jit(solution)/shard_map/ppermute | solution.py:23
  32.9 2.7 %collective-permute-start.5 = (bf16[8,8,768]{2,1,0:T(8,128)(2,1)S(1)}, bf16[8,8,768]{2,1,0:T(8,128)(2,1)S(1)}, u32[]{:S(2)}, u32[]{:S(2)}) collective-permute-start(bf16[8,8,768]{2,1,0:T(8,128)(2,1)S(1)} %collective-permute-done.3), channel_id=1, source_target_pairs={{0,7},{1,0},{2,1},{3,2},{4,3},{5,4},{6,5},{7,6},{8,15},{9,8},{10,9... | collective-permute-start | bytes 294920 | tf_op jit(solution)/shard_map/ppermute | solution.py:23
  35.6 2.2 %collective-permute-done.4 = bf16[8,8,768]{2,1,0:T(8,128)(2,1)S(1)} collective-permute-done((bf16[8,8,768]{2,1,0:T(8,128)(2,1)S(1)}, bf16[8,8,768]{2,1,0:T(8,128)(2,1)S(1)}, u32[]{:S(2)}, u32[]{:S(2)}) %collective-permute-start.4) | collective-permute-done | bytes 98336 | tf_op jit(solution)/shard_map/ppermute | solution.py:23
  37.9 2.7 %collective-permute-start.7 = (bf16[4,8,768]{2,1,0:T(8,128)(2,1)S(1)}, bf16[4,8,768]{2,1,0:T(8,128)(2,1)S(1)}, u32[]{:S(2)}, u32[]{:S(2)}) collective-permute-start(bf16[4,8,768]{2,1,0:T(8,128)(2,1)S(1)} %slice.22), channel_id=1, source_target_pairs={{0,7},{1,0},{2,1},{3,2},{4,3},{5,4},{6,5},{7,6},{8,15},{9,8},{10,9... | collective-permute-start | bytes 147464 | tf_op jit(solution)/shard_map/ppermute | solution.py:23
  47.8 3.4 %collective-permute-done.8.refs_2_ = bf16[4,8,8,768]{3,2,1,0:T(8,128)(2,1)S(1)} collective-permute-done((bf16[4,8,8,768]{3,2,1,0:T(8,128)(2,1)S(1)}, bf16[4,8,8,768]{3,2,1,0:T(8,128)(2,1)S(1)}, u32[]{:S(2)}, u32[]{:S(2)}) %collective-permute-start.8) | collective-permute-done | bytes 393248 | tf_op jit(solution)/shard_map/ppermute | solution.py:23
  51.2 2.8 %collective-permute-start.13 = (bf16[4,8,8,768]{3,2,1,0:T(8,128)(2,1)S(1)}, bf16[4,8,8,768]{3,2,1,0:T(8,128)(2,1)}, u32[]{:S(2)}, u32[]{:S(2)}) collective-permute-start(bf16[4,8,8,768]{3,2,1,0:T(8,128)(2,1)S(1)} %collective-permute-done.11.refs_5_), channel_id=1, source_target_pairs={{0,24},{8,0},{16,8},{24,16},{1,25},{9,1},{17,9},{25,17},{2,26},{10... | collective-permute-start | bytes 1179656 | tf_op jit(solution)/shard_map/ppermute | solution.py:23
  59.6 8.5 %collective-permute-done.12.refs_6_ = bf16[4,8,8,768]{3,2,1,0:T(8,128)(2,1)S(1)} collective-permute-done((bf16[4,8,8,768]{3,2,1,0:T(8,128)(2,1)S(1)}, bf16[4,8,8,768]{3,2,1,0:T(8,128)(2,1)S(1)}, u32[]{:S(2)}, u32[]{:S(2)}) %collective-permute-start.12) | collective-permute-done | bytes 393248 | tf_op jit(solution)/shard_map/ppermute | solution.py:23
  68.2 4.4 %proj.1 = (bf16[4,384,256]{2,1,0:T(8,128)(2,1)}, bf16[768,256]{1,0:T(8,128)(2,1)S(1)}) custom-call(s32[4]{0:T(128)S(1)} %pad_add_fusion.pos, bf16[8,384,256]{2,1,0:T(8,128)(2,1)S(1)} %norm.1.normed, f32[1,768]{1,0:T(1,128)S(1)} %reshape.70.bias, f32[384,128]{1,0:T(8,128)S(1)} %get-tuple-element.65.cosw, f32[384,128]{1,0:T(8,128)S(1)} %get-tuple-element.64.sinl, ...), custom_call_target="tpu_custom_call" | custom-call | tf_op jit(solution)/shard_map/proj/pallas_call | solution.py:130
  73.4 3.6 %all-to-all-start.1 = ((bf16[4,384,256]{2,1,0:T(8,128)(2,1)}), bf16[4,384,256]{2,1,0:T(8,128)(2,1)S(1)}, u32[]{:S(2)}, u32[]{:S(2)}) async-start(bf16[4,384,256]{2,1,0:T(8,128)(2,1)} %get-tuple-element.34), calls=%async_computation.1 | async-start | bytes 1572864 | tf_op jit(solution)/shard_map/all_to_all | solution.py:410
  77.2 2.7 %collective-permute-start.16 = (bf16[768,256]{1,0:T(8,128)(2,1)S(1)}, bf16[768,256]{1,0:T(8,128)(2,1)}, u32[]{:S(2)}, u32[]{:S(2)}) collective-permute-start(bf16[768,256]{1,0:T(8,128)(2,1)S(1)} %copy-done.5), channel_id=1, source_target_pairs={{0,7},{1,0},{2,1},{3,2},{4,3},{5,4},{6,5},{7,6},{8,15},{9,8},{10,9... | collective-permute-start | bytes 1179656 | tf_op jit(solution)/shard_map/ppermute | solution.py:23
  79.8 5.6 %all-to-all-done.1.q = bf16[4,384,256]{2,1,0:T(8,128)(2,1)S(1)} async-done(((bf16[4,384,256]{2,1,0:T(8,128)(2,1)}), bf16[4,384,256]{2,1,0:T(8,128)(2,1)S(1)}, u32[]{:S(2)}, u32[]{:S(2)}) %all-to-all-start.1) | async-done | bytes 786464 | tf_op jit(solution)/shard_map/all_to_all | solution.py:410
  87.3 3.6 %collective-permute-done.14.refs_1_ = bf16[768,256]{1,0:T(8,128)(2,1)S(1)} collective-permute-done((bf16[768,256]{1,0:T(8,128)(2,1)S(1)}, bf16[768,256]{1,0:T(8,128)(2,1)S(1)}, u32[]{:S(2)}, u32[]{:S(2)}) %collective-permute-start.14) | collective-permute-done | bytes 393248 | tf_op jit(solution)/shard_map/ppermute | solution.py:23
  93.6 9.0 %attend.4 = (f32[4,256,384]{2,1,0:T(8,128)S(1)}, f32[4,8,384]{2,1,0:T(8,128)S(1)}) custom-call(s32[4]{0:T(128)S(1)} %pad_add_fusion.pos, s32[8]{0:T(128)S(1)} %copy-done.8, s32[8]{0:T(128)S(1)} %copy-done.9, s32[8]{0:T(128)S(1)} %copy-done.12, bf16[4,384,256]{2,1,0:T(8,128)(2,1)S(1)} %all-to-all-done.1.q, bf16[768,256]{1,0:T(8,128)(2,1)S(1)} %copy-done.5, ...), custom_call_target="tpu_custom_call" | custom-call | tf_op jit(solution)/shard_map/attend/pallas_call | solution.py:292
  102.7 2.7 %collective-permute-start.19 = (bf16[768,256]{1,0:T(8,128)(2,1)S(1)}, bf16[768,256]{1,0:T(8,128)(2,1)S(1)}, u32[]{:S(2)}, u32[]{:S(2)}) collective-permute-start(bf16[768,256]{1,0:T(8,128)(2,1)S(1)} %collective-permute-done.17.refs_1_), channel_id=1, source_target_pairs={{0,7},{1,0},{2,1},{3,2},{4,3},{5,4},{6,5},{7,6},{8,15},{9,8},{10,9... | collective-permute-start | bytes 1179656 | tf_op jit(solution)/shard_map/ppermute | solution.py:23
  105.4 5.7 %attend.5 = (f32[4,256,384]{2,1,0:T(8,128)S(1)}, f32[4,8,384]{2,1,0:T(8,128)S(1)}) custom-call(s32[4]{0:T(128)S(1)} %pad_add_fusion.pos, s32[8]{0:T(128)S(1)} %copy-done.8, s32[8]{0:T(128)S(1)} %copy-done.9, s32[8]{0:T(128)S(1)} %copy-done.12, bf16[4,384,256]{2,1,0:T(8,128)(2,1)S(1)} %all-to-all-done.1.q, ...), custom_call_target="tpu_custom_call", output_to_operand_aliasing={{0}: (7, {}), {1}: (8, {})} | custom-call | tf_op jit(solution)/shard_map/attend/pallas_call | solution.py:292
  112.9 6.5 %attend.6 = (f32[4,256,384]{2,1,0:T(8,128)S(1)}, f32[4,8,384]{2,1,0:T(8,128)S(1)}) custom-call(s32[4]{0:T(128)S(1)} %pad_add_fusion.pos, s32[8]{0:T(128)S(1)} %copy-done.8, s32[8]{0:T(128)S(1)} %copy-done.9, s32[8]{0:T(128)S(1)} %copy-done.12, bf16[4,384,256]{2,1,0:T(8,128)(2,1)S(1)} %all-to-all-done.1.q, ...), custom_call_target="tpu_custom_call", output_to_operand_aliasing={{0}: (8, {}), {1}: (9, {})} | custom-call | tf_op jit(solution)/shard_map/attend/pallas_call | solution.py:292
  119.5 3.6 %attend.7 = bf16[4,272,384]{2,1,0:T(8,128)(2,1)S(1)} custom-call(s32[4]{0:T(128)S(1)} %pad_add_fusion.pos, s32[8]{0:T(128)S(1)} %copy-done.8, s32[8]{0:T(128)S(1)} %copy-done.9, s32[8]{0:T(128)S(1)} %copy-done.12, bf16[4,384,256]{2,1,0:T(8,128)(2,1)S(1)} %all-to-all-done.1.q, bf16[768,256]{1,0:T(8,128)(2,1)} %collective-permute-done.20.refs_0_, ...), custom_call_target="tpu_custom_call" | custom-call | tf_op jit(solution)/shard_map/attend/pallas_call | solution.py:292
  124.8 3.2 %collective-permute-done.21.b = bf16[272,384]{1,0:T(8,128)(2,1)S(1)} collective-permute-done((bf16[272,384]{1,0:T(8,128)(2,1)S(1)}, bf16[272,384]{1,0:T(8,128)(2,1)S(1)}, u32[]{:S(2)}, u32[]{:S(2)}) %collective-permute-start.21) | collective-permute-done | bytes 208928 | tf_op jit(solution)/shard_map/ppermute | solution.py:23
  127.9 3.5 %collective-permute-done.22.c = bf16[272,384]{1,0:T(8,128)(2,1)S(1)} collective-permute-done((bf16[272,384]{1,0:T(8,128)(2,1)S(1)}, bf16[272,384]{1,0:T(8,128)(2,1)S(1)}, u32[]{:S(2)}, u32[]{:S(2)}) %collective-permute-start.22) | collective-permute-done | bytes 208928 | tf_op jit(solution)/shard_map/ppermute | solution.py:23
  131.8 12.9 %all_to_all.16.mine = bf16[4,384,256]{2,1,0:T(8,128)(2,1)S(1)} all-to-all(bf16[4,384,256]{2,1,0:T(8,128)(2,1)S(1)} %combine.1), channel_id=1, replica_groups=mesh['x'=4,'c'=2,'y'=4,'z'=8] {'x'}, dimensions={0} | all-to-all | bytes 1572864 | tf_op jit(solution)/shard_map/all_to_all | solution.py:428
  144.7 7.1 %collective-permute-start.24 = (bf16[4,384,256]{2,1,0:T(8,128)(2,1)S(1)}, bf16[4,384,256]{2,1,0:T(8,128)(2,1)S(1)}, u32[]{:S(2)}, u32[]{:S(2)}) collective-permute-start(bf16[4,384,256]{2,1,0:T(8,128)(2,1)S(1)} %all_to_all.16.mine), channel_id=1, source_target_pairs={{0,32},{32,0},{1,33},{33,1},{2,34},{34,2},{3,35},{35,3},{4,36},{36... | collective-permute-start | bytes 2359304 | tf_op jit(solution)/shard_map/ppermute | solution.py:429
  (107 shorter events, 31.9 us)
Async XLA Ops:
  6.5 48.4 %all-gather.8.cloned.1.call-start = ((), (), s32[]{:S(2)}) async-start(), calls=%async_computation.4 | async-start | bytes 1769472 | tf_op jit(solution)/shard_map/all_gather | solution.py:404
  7.3 78.4 %all-gather.10.cloned.1.call-start = ((), (), s32[]{:S(2)}) async-start(), calls=%async_computation.5 | async-start | bytes 2654208 | tf_op jit(solution)/shard_map/all_gather | solution.py:403
  20.2 7.6 %collective-permute-start = (bf16[8,8,768]{2,1,0:T(8,128)(2,1)S(1)}, bf16[8,8,768]{2,1,0:T(8,128)(2,1)S(1)}, u32[]{:S(2)}, u32[]{:S(2)}) collective-permute-start(bf16[8,8,768]{2,1,0:T(8,128)(2,1)S(1)} %slice.20), channel_id=1, source_target_pairs={{0,1},{1,2},{2,3},{3,4},{4,5},{5,6},{6,7},{7,0},{8,9},{9,10},{10,1... | collective-permute-start | bytes 294920 | tf_op jit(solution)/shard_map/ppermute | solution.py:23
  21.9 6.0 %collective-permute-start.1 = (bf16[8,8,768]{2,1,0:T(8,128)(2,1)S(1)}, bf16[8,8,768]{2,1,0:T(8,128)(2,1)S(1)}, u32[]{:S(2)}, u32[]{:S(2)}) collective-permute-start(bf16[8,8,768]{2,1,0:T(8,128)(2,1)S(1)} %slice.20), channel_id=1, source_target_pairs={{0,7},{1,0},{2,1},{3,2},{4,3},{5,4},{6,5},{7,6},{8,15},{9,8},{10,9... | collective-permute-start | bytes 294920 | tf_op jit(solution)/shard_map/ppermute | solution.py:23
  27.8 5.1 %collective-permute-start.2 = (bf16[8,8,768]{2,1,0:T(8,128)(2,1)S(1)}, bf16[8,8,768]{2,1,0:T(8,128)(2,1)S(1)}, u32[]{:S(2)}, u32[]{:S(2)}) collective-permute-start(bf16[8,8,768]{2,1,0:T(8,128)(2,1)S(1)} %collective-permute-done), channel_id=1, source_target_pairs={{0,1},{1,2},{2,3},{3,4},{4,5},{5,6},{6,7},{7,0},{8,9},{9,10},{10,1... | collective-permute-start | bytes 294920 | tf_op jit(solution)/shard_map/ppermute | solution.py:23
  27.8 5.1 %collective-permute-start.3 = (bf16[8,8,768]{2,1,0:T(8,128)(2,1)S(1)}, bf16[8,8,768]{2,1,0:T(8,128)(2,1)S(1)}, u32[]{:S(2)}, u32[]{:S(2)}) collective-permute-start(bf16[8,8,768]{2,1,0:T(8,128)(2,1)S(1)} %collective-permute-done.1), channel_id=1, source_target_pairs={{0,7},{1,0},{2,1},{3,2},{4,3},{5,4},{6,5},{7,6},{8,15},{9,8},{10,9... | collective-permute-start | bytes 294920 | tf_op jit(solution)/shard_map/ppermute | solution.py:23
  43.1 8.1 %collective-permute-start.8 = (bf16[4,8,8,768]{3,2,1,0:T(8,128)(2,1)S(1)}, bf16[4,8,8,768]{3,2,1,0:T(8,128)(2,1)S(1)}, u32[]{:S(2)}, u32[]{:S(2)}) collective-permute-start(bf16[4,8,8,768]{3,2,1,0:T(8,128)(2,1)S(1)} %bitcast.29), channel_id=1, source_target_pairs={{0,8},{8,16},{16,24},{24,0},{1,9},{9,17},{17,25},{25,1},{2,10},{10... | collective-permute-start | bytes 1179656 | tf_op jit(solution)/shard_map/ppermute | solution.py:23
  44.4 6.8 %collective-permute-start.11 = (bf16[4,8,8,768]{3,2,1,0:T(8,128)(2,1)S(1)}, bf16[4,8,8,768]{3,2,1,0:T(8,128)(2,1)S(1)}, u32[]{:S(2)}, u32[]{:S(2)}) collective-permute-start(bf16[4,8,8,768]{3,2,1,0:T(8,128)(2,1)S(1)} %bitcast.32), channel_id=1, source_target_pairs={{0,24},{8,0},{16,8},{24,16},{1,25},{9,1},{17,9},{25,17},{2,26},{10... | collective-permute-start | bytes 1179656 | tf_op jit(solution)/shard_map/ppermute | solution.py:23
  46.2 12.4 %collective-permute-start.10 = (bf16[4,8,8,768]{3,2,1,0:T(8,128)(2,1)S(1)}, bf16[4,8,8,768]{3,2,1,0:T(8,128)(2,1)S(1)}, u32[]{:S(2)}, u32[]{:S(2)}) collective-permute-start(bf16[4,8,8,768]{3,2,1,0:T(8,128)(2,1)S(1)} %bitcast.30), channel_id=1, source_target_pairs={{0,24},{8,0},{16,8},{24,16},{1,25},{9,1},{17,9},{25,17},{2,26},{10... | collective-permute-start | bytes 1179656 | tf_op jit(solution)/shard_map/ppermute | solution.py:23
  47.7 11.9 %collective-permute-start.9 = (bf16[4,8,8,768]{3,2,1,0:T(8,128)(2,1)S(1)}, bf16[4,8,8,768]{3,2,1,0:T(8,128)(2,1)S(1)}, u32[]{:S(2)}, u32[]{:S(2)}) collective-permute-start(bf16[4,8,8,768]{3,2,1,0:T(8,128)(2,1)S(1)} %bitcast.33), channel_id=1, source_target_pairs={{0,8},{8,16},{16,24},{24,0},{1,9},{9,17},{17,25},{25,1},{2,10},{10... | collective-permute-start | bytes 1179656 | tf_op jit(solution)/shard_map/ppermute | solution.py:23
  51.2 16.9 %collective-permute-start.12 = (bf16[4,8,8,768]{3,2,1,0:T(8,128)(2,1)S(1)}, bf16[4,8,8,768]{3,2,1,0:T(8,128)(2,1)S(1)}, u32[]{:S(2)}, u32[]{:S(2)}) collective-permute-start(bf16[4,8,8,768]{3,2,1,0:T(8,128)(2,1)S(1)} %collective-permute-done.8.refs_2_), channel_id=1, source_target_pairs={{0,8},{8,16},{16,24},{24,0},{1,9},{9,17},{17,25},{25,1},{2,10},{10... | collective-permute-start | bytes 1179656 | tf_op jit(solution)/shard_map/ppermute | solution.py:23
  51.2 16.9 %collective-permute-start.13 = (bf16[4,8,8,768]{3,2,1,0:T(8,128)(2,1)S(1)}, bf16[4,8,8,768]{3,2,1,0:T(8,128)(2,1)}, u32[]{:S(2)}, u32[]{:S(2)}) collective-permute-start(bf16[4,8,8,768]{3,2,1,0:T(8,128)(2,1)S(1)} %collective-permute-done.11.refs_5_), channel_id=1, source_target_pairs={{0,24},{8,0},{16,8},{24,16},{1,25},{9,1},{17,9},{25,17},{2,26},{10... | collective-permute-start | bytes 1179656 | tf_op jit(solution)/shard_map/ppermute | solution.py:23
  73.4 12.0 %all-to-all-start.1 = ((bf16[4,384,256]{2,1,0:T(8,128)(2,1)}), bf16[4,384,256]{2,1,0:T(8,128)(2,1)S(1)}, u32[]{:S(2)}, u32[]{:S(2)}) async-start(bf16[4,384,256]{2,1,0:T(8,128)(2,1)} %get-tuple-element.34), calls=%async_computation.1 | async-start | bytes 1572864 | tf_op jit(solution)/shard_map/all_to_all | solution.py:410
  77.0 42.4 %all-gather.6.cloned.1.call-start = ((), (), s32[]{:S(2)}) async-start(), calls=%async_computation.3 | async-start | bytes 1310720 | tf_op jit(solution)/shard_map/all_gather | solution.py:413
  77.1 13.9 %collective-permute-start.14 = (bf16[768,256]{1,0:T(8,128)(2,1)S(1)}, bf16[768,256]{1,0:T(8,128)(2,1)S(1)}, u32[]{:S(2)}, u32[]{:S(2)}) collective-permute-start(bf16[768,256]{1,0:T(8,128)(2,1)S(1)} %copy-done.5), channel_id=1, source_target_pairs={{0,1},{1,2},{2,3},{3,4},{4,5},{5,6},{6,7},{7,0},{8,9},{9,10},{10,1... | collective-permute-start | bytes 1179656 | tf_op jit(solution)/shard_map/ppermute | solution.py:23
  77.2 14.8 %collective-permute-start.16 = (bf16[768,256]{1,0:T(8,128)(2,1)S(1)}, bf16[768,256]{1,0:T(8,128)(2,1)}, u32[]{:S(2)}, u32[]{:S(2)}) collective-permute-start(bf16[768,256]{1,0:T(8,128)(2,1)S(1)} %copy-done.5), channel_id=1, source_target_pairs={{0,7},{1,0},{2,1},{3,2},{4,3},{5,4},{6,5},{7,6},{8,15},{9,8},{10,9... | collective-permute-start | bytes 1179656 | tf_op jit(solution)/shard_map/ppermute | solution.py:23
  90.9 11.7 %collective-permute-start.15 = (bf16[768,256]{1,0:T(8,128)(2,1)S(1)}, bf16[768,256]{1,0:T(8,128)(2,1)S(1)}, u32[]{:S(2)}, u32[]{:S(2)}) collective-permute-start(bf16[768,256]{1,0:T(8,128)(2,1)S(1)} %collective-permute-done.14.refs_1_), channel_id=1, source_target_pairs={{0,1},{1,2},{2,3},{3,4},{4,5},{5,6},{6,7},{7,0},{8,9},{9,10},{10,1... | collective-permute-start | bytes 1179656 | tf_op jit(solution)/shard_map/ppermute | solution.py:23
  91.9 10.7 %collective-permute-start.17 = (bf16[768,256]{1,0:T(8,128)(2,1)}, bf16[768,256]{1,0:T(8,128)(2,1)S(1)}, u32[]{:S(2)}, u32[]{:S(2)}) collective-permute-start(bf16[768,256]{1,0:T(8,128)(2,1)} %collective-permute-done.16.refs_2_), channel_id=1, source_target_pairs={{0,7},{1,0},{2,1},{3,2},{4,3},{5,4},{6,5},{7,6},{8,15},{9,8},{10,9... | collective-permute-start | bytes 1179656 | tf_op jit(solution)/shard_map/ppermute | solution.py:23
  102.6 8.5 %collective-permute-start.18 = (bf16[768,256]{1,0:T(8,128)(2,1)S(1)}, bf16[768,256]{1,0:T(8,128)(2,1)S(1)}, u32[]{:S(2)}, u32[]{:S(2)}) collective-permute-start(bf16[768,256]{1,0:T(8,128)(2,1)S(1)} %collective-permute-done.15.refs_0_), channel_id=1, source_target_pairs={{0,1},{1,2},{2,3},{3,4},{4,5},{5,6},{6,7},{7,0},{8,9},{9,10},{10,1... | collective-permute-start | bytes 1179656 | tf_op jit(solution)/shard_map/ppermute | solution.py:23
  102.7 8.4 %collective-permute-start.19 = (bf16[768,256]{1,0:T(8,128)(2,1)S(1)}, bf16[768,256]{1,0:T(8,128)(2,1)S(1)}, u32[]{:S(2)}, u32[]{:S(2)}) collective-permute-start(bf16[768,256]{1,0:T(8,128)(2,1)S(1)} %collective-permute-done.17.refs_1_), channel_id=1, source_target_pairs={{0,7},{1,0},{2,1},{3,2},{4,3},{5,4},{6,5},{7,6},{8,15},{9,8},{10,9... | collective-permute-start | bytes 1179656 | tf_op jit(solution)/shard_map/ppermute | solution.py:23
  111.1 8.3 %collective-permute-start.20 = (bf16[768,256]{1,0:T(8,128)(2,1)S(1)}, bf16[768,256]{1,0:T(8,128)(2,1)}, u32[]{:S(2)}, u32[]{:S(2)}) collective-permute-start(bf16[768,256]{1,0:T(8,128)(2,1)S(1)} %collective-permute-done.18.refs_0_), channel_id=1, source_target_pairs={{0,1},{1,2},{2,3},{3,4},{4,5},{5,6},{6,7},{7,0},{8,9},{9,10},{10,1... | collective-permute-start | bytes 1179656 | tf_op jit(solution)/shard_map/ppermute | solution.py:23
  123.3 8.2 %collective-permute-start.22 = (bf16[272,384]{1,0:T(8,128)(2,1)S(1)}, bf16[272,384]{1,0:T(8,128)(2,1)S(1)}, u32[]{:S(2)}, u32[]{:S(2)}) collective-permute-start(bf16[272,384]{1,0:T(8,128)(2,1)S(1)} %get-tuple-element.60), channel_id=1, source_target_pairs={{0,8},{8,16},{16,24},{24,0},{1,9},{9,17},{17,25},{25,1},{2,10},{10... | collective-permute-start | bytes 626696 | tf_op jit(solution)/shard_map/ppermute | solution.py:23
  124.8 6.7 %collective-permute-start.23 = (bf16[272,384]{1,0:T(8,128)(2,1)S(1)}, bf16[272,384]{1,0:T(8,128)(2,1)S(1)}, u32[]{:S(2)}, u32[]{:S(2)}) collective-permute-start(bf16[272,384]{1,0:T(8,128)(2,1)S(1)} %get-tuple-element.59), channel_id=1, source_target_pairs={{0,16},{8,24},{16,0},{24,8},{1,17},{9,25},{17,1},{25,9},{2,18},{10... | collective-permute-start | bytes 626696 | tf_op jit(solution)/shard_map/ppermute | solution.py:23
  144.7 9.1 %collective-permute-start.24 = (bf16[4,384,256]{2,1,0:T(8,128)(2,1)S(1)}, bf16[4,384,256]{2,1,0:T(8,128)(2,1)S(1)}, u32[]{:S(2)}, u32[]{:S(2)}) collective-permute-start(bf16[4,384,256]{2,1,0:T(8,128)(2,1)S(1)} %all_to_all.16.mine), channel_id=1, source_target_pairs={{0,32},{32,0},{1,33},{33,1},{2,34},{34,2},{3,35},{35,3},{4,36},{36... | collective-permute-start | bytes 2359304 | tf_op jit(solution)/shard_map/ppermute | solution.py:429
  (22 other events, 349.2 us)
Sparse Core Ops, SparseCore 0:
  9.2 31.0 all-gather.7
  43.0 42.6 all-gather.9
  87.5 29.3 all-gather.5
where the time goes:
time: 161 us; the launch traced here: 162 us
  starting transfers between devices  41.8 us (26%)
  waiting for transfers between devices  40.3 us (25%)
  Pallas kernels  33 us (20%)
  blocking collectives  24 us (15%)
  between operations  13.5 us (8%)
  local copies, waits for them, and re-layouts  7.48 us (5%)
  other arithmetic  2.04 us (1%)
    ppermute x24, waiting for transfers between devices, shift(): return lax.ppermute(value, axis, [(i, (i + by) % n) for i in range(n)])  31.8 us
    ppermute x24, starting transfers between devices, shift(): return lax.ppermute(value, axis, [(i, (i + by) % n) for i in range(n)])  31 us
    pallas_call x4, Pallas kernels, attend_call(): pl.pallas_call(kernel, out_shape=out_shape, in_specs=[smem()] * 4 + specs...  24.8 us
    all_to_all x1, blocking collectives, shards(): a_mine = lax.all_to_all(combine_call(back), 'x', 0, 0, tiled=True)  12.9 us
    all_to_all x1, blocking collectives, shards(): wide = lax.all_to_all(prep_call(w_qkv, w_out), ('x', 'c'), 0, 0, tiled=True)  11 us
    ppermute x1, starting transfers between devices, shards(): a_other = lax.ppermute(a_mine, 'c', [(0, 1), (1, 0)])  7.14 us
    unnamed x38, local copies, waits for them, and re-layouts  5.66 us
    all_to_all x1, waiting for transfers between devices, shards(): q = lax.all_to_all(q4, 'y', 0, 0, tiled=True)  5.56 us
  transfers between devices with their start and end apart: 29, of which 14 were waited for; matrix products, arithmetic and copies ran while one was open for 2% of the time, Pallas kernels for 17%

commit v1 on v0

--- a/solution.py
+++ b/solution.py
@@ -408,14 +408,13 @@
 
     q4, kv = proj_call(pos, normed, qkv_bias.reshape(1, 3 * HD), tables, w_blocks)
     q = lax.all_to_all(q4, "y", 0, 0, tiled=True)
-    q, table = lax.optimization_barrier((q, table))
-    w_o = table[:, 2 * slots :].reshape(NZ, NX * NC, 8, HD)
-    w_o = lax.all_gather(w_o, "y", axis=0, tiled=False)
     meta = (pos, plen, clen, hold, q)
     r1, l1 = shift(kv, "z", 1), shift(kv, "z", -1)
     r2, l2 = shift(r1, "z", 1), shift(l1, "z", -1)
     state = attend_call(*meta, [kv, r1, l1], (0, -1, 1))
-    r2, l2, state = lax.optimization_barrier((r2, l2, state))
+    r2, l2, state, table = lax.optimization_barrier((r2, l2, state, table))
+    w_o = table[:, 2 * slots :].reshape(NZ, NX * NC, 8, HD)
+    w_o = lax.all_gather(w_o, "y", axis=0, tiled=False)
     r3, l3 = shift(r2, "z", 1), shift(l2, "z", -1)
     state = attend_call(*meta, [r2, l2], (-2, 2), state=state)
     r3, l3, state = lax.optimization_barrier((r3, l3, state))

time: 161 us -> 172 us (1.068); the launches traced: 162 us -> 171 us
  waiting for transfers between devices: 40.3 us -> 55.1 us
  Pallas kernels: 33 us -> 30.5 us
  starting transfers between devices: 41.8 us -> 39.7 us
    ppermute x24, waiting for transfers between devices: 31.8 us -> 43.2 us  [shift(): return lax.ppermute(value, axis, [(i, (i + by) % n) for i in range(n)])]
    all_gather x1, waiting for transfers between devices: 0.02 us -> 9.27 us  [shards(): w_o = lax.all_gather(w_o, 'y', axis=0, tiled=False)]
    all_to_all x1, waiting for transfers between devices: 5.56 us -> 0.01 us  [shards(): q = lax.all_to_all(q4, 'y', 0, 0, tiled=True)]
    pallas_call x4, Pallas kernels: 24.8 us -> 22.1 us  [attend_call(): pl.pallas_call(kernel, out_shape=out_shape, in_specs=[smem()] * 4 + specs...]
    ppermute x1, starting transfers between devices: 7.14 us -> 4.8 us  [shards(): a_other = lax.ppermute(a_mine, 'c', [(0, 1), (1, 0)])]
    unnamed x38 -> x34, local copies, waits for them, and re-layouts: 5.66 us -> 4.9 us
  transfers between devices with their start and end apart: 29 -> 29, of which waited for: 14 -> 15; matrix products, arithmetic and copies ran while one was open for 2% -> 1% of each run, Pallas kernels for 17% -> 15%
where the time goes in v1:
time: 172 us; the launch traced here: 171 us
  waiting for transfers between devices  55.1 us (32%)
  starting transfers between devices  39.7 us (23%)
  Pallas kernels  30.5 us (18%)
  blocking collectives  23.4 us (14%)
  between operations  13.5 us (8%)
  local copies, waits for them, and re-layouts  6.72 us (4%)
  other arithmetic  2.06 us (1%)
    ppermute x24, waiting for transfers between devices, shift(): return lax.ppermute(value, axis, [(i, (i + by) % n) for i in range(n)])  43.2 us
    ppermute x24, starting transfers between devices, shift(): return lax.ppermute(value, axis, [(i, (i + by) % n) for i in range(n)])  31.3 us
    pallas_call x4, Pallas kernels, attend_call(): pl.pallas_call(kernel, out_shape=out_shape, in_specs=[smem()] * 4 + specs...  22.1 us
    all_to_all x1, blocking collectives, shards(): a_mine = lax.all_to_all(combine_call(back), 'x', 0, 0, tiled=True)  12.3 us
    all_to_all x1, blocking collectives, shards(): wide = lax.all_to_all(prep_call(w_qkv, w_out), ('x', 'c'), 0, 0, tiled=True)  11 us
    all_gather x1, waiting for transfers between devices, shards(): w_o = lax.all_gather(w_o, 'y', axis=0, tiled=False)  9.27 us
    unnamed x34, local copies, waits for them, and re-layouts  4.9 us
    ppermute x1, starting transfers between devices, shards(): a_other = lax.ppermute(a_mine, 'c', [(0, 1), (1, 0)])  4.8 us
  transfers between devices with their start and end apart: 29, of which 15 were waited for; matrix products, arithmetic and copies ran while one was open for 1% of the time, Pallas kernels for 15%

profile of v1, /device:TPU:1, one launch (start us, length us, event | category | flops | bytes accessed | tf_op | source)
XLA Modules:
  0.0 171.0 jit_solution(3168239274110215293)
XLA Ops:
  9.1 11.0 %all_to_all.15 = bf16[8,8,1024]{2,1,0:T(8,128)(2,1)S(1)} all-to-all(bf16[8,8,1024]{2,1,0:T(8,128)(2,1)S(1)} %prep.1), channel_id=1, replica_groups=mesh['x'=4,'c'=2,'y'=4,'z'=8] {'x','c'}, dimensions={0} | all-to-all | bytes 262144 | tf_op jit(solution)/shard_map/all_to_all | solution.py:396
  21.9 4.0 %collective-permute-start.1 = (bf16[8,8,768]{2,1,0:T(8,128)(2,1)S(1)}, bf16[8,8,768]{2,1,0:T(8,128)(2,1)S(1)}, u32[]{:S(2)}, u32[]{:S(2)}) collective-permute-start(bf16[8,8,768]{2,1,0:T(8,128)(2,1)S(1)} %slice.20), channel_id=1, source_target_pairs={{0,7},{1,0},{2,1},{3,2},{4,3},{5,4},{6,5},{7,6},{8,15},{9,8},{10,9... | collective-permute-start | bytes 294920 | tf_op jit(solution)/shard_map/ppermute | solution.py:23
  27.8 2.8 %collective-permute-start.3 = (bf16[8,8,768]{2,1,0:T(8,128)(2,1)S(1)}, bf16[8,8,768]{2,1,0:T(8,128)(2,1)S(1)}, u32[]{:S(2)}, u32[]{:S(2)}) collective-permute-start(bf16[8,8,768]{2,1,0:T(8,128)(2,1)S(1)} %collective-permute-done.1), channel_id=1, source_target_pairs={{0,7},{1,0},{2,1},{3,2},{4,3},{5,4},{6,5},{7,6},{8,15},{9,8},{10,9... | collective-permute-start | bytes 294920 | tf_op jit(solution)/shard_map/ppermute | solution.py:23
  32.9 2.7 %collective-permute-start.5 = (bf16[8,8,768]{2,1,0:T(8,128)(2,1)S(1)}, bf16[8,8,768]{2,1,0:T(8,128)(2,1)S(1)}, u32[]{:S(2)}, u32[]{:S(2)}) collective-permute-start(bf16[8,8,768]{2,1,0:T(8,128)(2,1)S(1)} %collective-permute-done.3), channel_id=1, source_target_pairs={{0,7},{1,0},{2,1},{3,2},{4,3},{5,4},{6,5},{7,6},{8,15},{9,8},{10,9... | collective-permute-start | bytes 294920 | tf_op jit(solution)/shard_map/ppermute | solution.py:23
  37.9 2.7 %collective-permute-start.7 = (bf16[4,8,768]{2,1,0:T(8,128)(2,1)S(1)}, bf16[4,8,768]{2,1,0:T(8,128)(2,1)S(1)}, u32[]{:S(2)}, u32[]{:S(2)}) collective-permute-start(bf16[4,8,768]{2,1,0:T(8,128)(2,1)S(1)} %slice.22), channel_id=1, source_target_pairs={{0,7},{1,0},{2,1},{3,2},{4,3},{5,4},{6,5},{7,6},{8,15},{9,8},{10,9... | collective-permute-start | bytes 147464 | tf_op jit(solution)/shard_map/ppermute | solution.py:23
  47.8 3.4 %collective-permute-done.8.refs_2_ = bf16[4,8,8,768]{3,2,1,0:T(8,128)(2,1)S(1)} collective-permute-done((bf16[4,8,8,768]{3,2,1,0:T(8,128)(2,1)S(1)}, bf16[4,8,8,768]{3,2,1,0:T(8,128)(2,1)S(1)}, u32[]{:S(2)}, u32[]{:S(2)}) %collective-permute-start.8) | collective-permute-done | bytes 393248 | tf_op jit(solution)/shard_map/ppermute | solution.py:23
  51.3 2.8 %collective-permute-start.13 = (bf16[4,8,8,768]{3,2,1,0:T(8,128)(2,1)S(1)}, bf16[4,8,8,768]{3,2,1,0:T(8,128)(2,1)}, u32[]{:S(2)}, u32[]{:S(2)}) collective-permute-start(bf16[4,8,8,768]{3,2,1,0:T(8,128)(2,1)S(1)} %collective-permute-done.11.refs_5_), channel_id=1, source_target_pairs={{0,24},{8,0},{16,8},{24,16},{1,25},{9,1},{17,9},{25,17},{2,26},{10... | collective-permute-start | bytes 1179656 | tf_op jit(solution)/shard_map/ppermute | solution.py:23
  59.6 8.5 %collective-permute-done.12.refs_6_ = bf16[4,8,8,768]{3,2,1,0:T(8,128)(2,1)S(1)} collective-permute-done((bf16[4,8,8,768]{3,2,1,0:T(8,128)(2,1)S(1)}, bf16[4,8,8,768]{3,2,1,0:T(8,128)(2,1)S(1)}, u32[]{:S(2)}, u32[]{:S(2)}) %collective-permute-start.12) | collective-permute-done | bytes 393248 | tf_op jit(solution)/shard_map/ppermute | solution.py:23
  68.2 4.6 %proj.1 = (bf16[4,384,256]{2,1,0:T(8,128)(2,1)}, bf16[768,256]{1,0:T(8,128)(2,1)}) custom-call(s32[4]{0:T(128)S(1)} %pad_add_fusion.pos, bf16[8,384,256]{2,1,0:T(8,128)(2,1)S(1)} %norm.1.normed, f32[1,768]{1,0:T(1,128)S(1)} %reshape.70.bias, f32[384,128]{1,0:T(8,128)S(1)} %get-tuple-element.63.cosw, f32[384,128]{1,0:T(8,128)S(1)} %get-tuple-element.62.sinl, ...), custom_call_target="tpu_custom_call" | custom-call | tf_op jit(solution)/shard_map/proj/pallas_call | solution.py:130
  72.9 2.7 %collective-permute-start.16 = (bf16[768,256]{1,0:T(8,128)(2,1)}, bf16[768,256]{1,0:T(8,128)(2,1)S(1)}, u32[]{:S(2)}, u32[]{:S(2)}) collective-permute-start(bf16[768,256]{1,0:T(8,128)(2,1)} %get-tuple-element.34.refs_0_), channel_id=1, source_target_pairs={{0,7},{1,0},{2,1},{3,2},{4,3},{5,4},{6,5},{7,6},{8,15},{9,8},{10,9... | collective-permute-start | bytes 1179656 | tf_op jit(solution)/shard_map/ppermute | solution.py:23
  75.6 3.5 %all-to-all-start.1 = ((bf16[4,384,256]{2,1,0:T(8,128)(2,1)}), bf16[4,384,256]{2,1,0:T(8,128)(2,1)S(1)}, u32[]{:S(2)}, u32[]{:S(2)}) async-start(bf16[4,384,256]{2,1,0:T(8,128)(2,1)} %get-tuple-element.33), calls=%async_computation.1 | async-start | bytes 1572864 | tf_op jit(solution)/shard_map/all_to_all | solution.py:410
  79.2 11.6 %collective-permute-done.14.refs_1_ = bf16[768,256]{1,0:T(8,128)(2,1)S(1)} collective-permute-done((bf16[768,256]{1,0:T(8,128)(2,1)}, bf16[768,256]{1,0:T(8,128)(2,1)S(1)}, u32[]{:S(2)}, u32[]{:S(2)}) %collective-permute-start.14) | collective-permute-done | bytes 393248 | tf_op jit(solution)/shard_map/ppermute | solution.py:23
  90.8 2.7 %collective-permute-start.17 = (bf16[768,256]{1,0:T(8,128)(2,1)S(1)}, bf16[768,256]{1,0:T(8,128)(2,1)}, u32[]{:S(2)}, u32[]{:S(2)}) collective-permute-start(bf16[768,256]{1,0:T(8,128)(2,1)S(1)} %collective-permute-done.16.refs_2_), channel_id=1, source_target_pairs={{0,7},{1,0},{2,1},{3,2},{4,3},{5,4},{6,5},{7,6},{8,15},{9,8},{10,9... | collective-permute-start | bytes 1179656 | tf_op jit(solution)/shard_map/ppermute | solution.py:23
  93.4 4.6 %attend.4 = (f32[4,256,384]{2,1,0:T(8,128)S(1)}, f32[4,8,384]{2,1,0:T(8,128)S(1)}) custom-call(s32[4]{0:T(128)S(1)} %pad_add_fusion.pos, s32[8]{0:T(128)S(1)} %copy-done.6, s32[8]{0:T(128)S(1)} %copy-done.7, s32[8]{0:T(128)S(1)} %copy-done.10, bf16[4,384,256]{2,1,0:T(8,128)(2,1)S(1)} %all-to-all-done.1.q, bf16[768,256]{1,0:T(8,128)(2,1)} %get-tuple-element.34.refs_0_, ...), custom_call_target="tpu_custom_call" | custom-call | tf_op jit(solution)/shard_map/attend/pallas_call | solution.py:292
  101.8 2.7 %collective-permute-start.19 = (bf16[768,256]{1,0:T(8,128)(2,1)}, bf16[768,256]{1,0:T(8,128)(2,1)S(1)}, u32[]{:S(2)}, u32[]{:S(2)}) collective-permute-start(bf16[768,256]{1,0:T(8,128)(2,1)} %collective-permute-done.17.refs_1_), channel_id=1, source_target_pairs={{0,7},{1,0},{2,1},{3,2},{4,3},{5,4},{6,5},{7,6},{8,15},{9,8},{10,9... | collective-permute-start | bytes 1179656 | tf_op jit(solution)/shard_map/ppermute | solution.py:23
  104.4 6.3 %attend.5 = (f32[4,256,384]{2,1,0:T(8,128)S(1)}, f32[4,8,384]{2,1,0:T(8,128)S(1)}) custom-call(s32[4]{0:T(128)S(1)} %pad_add_fusion.pos, s32[8]{0:T(128)S(1)} %copy-done.6, s32[8]{0:T(128)S(1)} %copy-done.7, s32[8]{0:T(128)S(1)} %copy-done.10, bf16[4,384,256]{2,1,0:T(8,128)(2,1)S(1)} %all-to-all-done.1.q, ...), custom_call_target="tpu_custom_call", output_to_operand_aliasing={{0}: (7, {}), {1}: (8, {})} | custom-call | tf_op jit(solution)/shard_map/attend/pallas_call | solution.py:292
  112.6 7.6 %attend.6 = (f32[4,256,384]{2,1,0:T(8,128)S(1)}, f32[4,8,384]{2,1,0:T(8,128)S(1)}) custom-call(s32[4]{0:T(128)S(1)} %pad_add_fusion.pos, s32[8]{0:T(128)S(1)} %copy-done.6, s32[8]{0:T(128)S(1)} %copy-done.7, s32[8]{0:T(128)S(1)} %copy-done.10, bf16[4,384,256]{2,1,0:T(8,128)(2,1)S(1)} %all-to-all-done.1.q, ...), custom_call_target="tpu_custom_call", output_to_operand_aliasing={{0}: (8, {}), {1}: (9, {})} | custom-call | tf_op jit(solution)/shard_map/attend/pallas_call | solution.py:292
  120.2 9.3 %all-gather.6.cloned.1.call-done.w = bf16[4,8,8,8,256]{4,3,2,1,0:T(8,128)(2,1)} async-done(((bf16[1,8,8,8,256]{4,3,2,1,0:T(8,128)(2,1)}), bf16[4,8,8,8,256]{4,3,2,1,0:T(8,128)(2,1)}) %all-gather.6.cloned.1.call-update) | async-done | bytes 1048592 | tf_op jit(solution)/shard_map/all_gather | solution.py:417
  129.5 3.6 %attend.7 = bf16[4,272,384]{2,1,0:T(8,128)(2,1)S(1)} custom-call(s32[4]{0:T(128)S(1)} %pad_add_fusion.pos, s32[8]{0:T(128)S(1)} %copy-done.6, s32[8]{0:T(128)S(1)} %copy-done.7, s32[8]{0:T(128)S(1)} %copy-done.10, bf16[4,384,256]{2,1,0:T(8,128)(2,1)S(1)} %all-to-all-done.1.q, bf16[768,256]{1,0:T(8,128)(2,1)} %collective-permute-done.20.refs_0_, ...), custom_call_target="tpu_custom_call" | custom-call | tf_op jit(solution)/shard_map/attend/pallas_call | solution.py:292
  135.1 3.2 %collective-permute-done.21.b = bf16[272,384]{1,0:T(8,128)(2,1)S(1)} collective-permute-done((bf16[272,384]{1,0:T(8,128)(2,1)S(1)}, bf16[272,384]{1,0:T(8,128)(2,1)S(1)}, u32[]{:S(2)}, u32[]{:S(2)}) %collective-permute-start.21) | collective-permute-done | bytes 208928 | tf_op jit(solution)/shard_map/ppermute | solution.py:23
  138.4 2.6 %collective-permute-done.22.c = bf16[272,384]{1,0:T(8,128)(2,1)S(1)} collective-permute-done((bf16[272,384]{1,0:T(8,128)(2,1)S(1)}, bf16[272,384]{1,0:T(8,128)(2,1)S(1)}, u32[]{:S(2)}, u32[]{:S(2)}) %collective-permute-start.22) | collective-permute-done | bytes 208928 | tf_op jit(solution)/shard_map/ppermute | solution.py:23
  140.9 2.4 %collective-permute-done.23.d = bf16[272,384]{1,0:T(8,128)(2,1)S(1)} collective-permute-done((bf16[272,384]{1,0:T(8,128)(2,1)S(1)}, bf16[272,384]{1,0:T(8,128)(2,1)S(1)}, u32[]{:S(2)}, u32[]{:S(2)}) %collective-permute-start.23) | collective-permute-done | bytes 208928 | tf_op jit(solution)/shard_map/ppermute | solution.py:23
  143.6 12.3 %all_to_all.16.mine = bf16[4,384,256]{2,1,0:T(8,128)(2,1)S(1)} all-to-all(bf16[4,384,256]{2,1,0:T(8,128)(2,1)S(1)} %combine.1), channel_id=1, replica_groups=mesh['x'=4,'c'=2,'y'=4,'z'=8] {'x'}, dimensions={0} | all-to-all | bytes 1572864 | tf_op jit(solution)/shard_map/all_to_all | solution.py:427
  155.9 4.8 %collective-permute-start.24 = (bf16[4,384,256]{2,1,0:T(8,128)(2,1)S(1)}, bf16[4,384,256]{2,1,0:T(8,128)(2,1)S(1)}, u32[]{:S(2)}, u32[]{:S(2)}) collective-permute-start(bf16[4,384,256]{2,1,0:T(8,128)(2,1)S(1)} %all_to_all.16.mine), channel_id=1, source_target_pairs={{0,32},{32,0},{1,33},{33,1},{2,34},{34,2},{3,35},{35,3},{4,36},{36... | collective-permute-start | bytes 2359304 | tf_op jit(solution)/shard_map/ppermute | solution.py:428
  (103 shorter events, 35.1 us)
Async XLA Ops:
  6.5 48.4 %all-gather.8.cloned.1.call-start = ((), (), s32[]{:S(2)}) async-start(), calls=%async_computation.4 | async-start | bytes 1769472 | tf_op jit(solution)/shard_map/all_gather | solution.py:404
  7.3 92.7 %all-gather.10.cloned.1.call-start = ((), (), s32[]{:S(2)}) async-start(), calls=%async_computation.5 | async-start | bytes 2654208 | tf_op jit(solution)/shard_map/all_gather | solution.py:403
  20.2 7.6 %collective-permute-start = (bf16[8,8,768]{2,1,0:T(8,128)(2,1)S(1)}, bf16[8,8,768]{2,1,0:T(8,128)(2,1)S(1)}, u32[]{:S(2)}, u32[]{:S(2)}) collective-permute-start(bf16[8,8,768]{2,1,0:T(8,128)(2,1)S(1)} %slice.20), channel_id=1, source_target_pairs={{0,1},{1,2},{2,3},{3,4},{4,5},{5,6},{6,7},{7,0},{8,9},{9,10},{10,1... | collective-permute-start | bytes 294920 | tf_op jit(solution)/shard_map/ppermute | solution.py:23
  21.9 6.0 %collective-permute-start.1 = (bf16[8,8,768]{2,1,0:T(8,128)(2,1)S(1)}, bf16[8,8,768]{2,1,0:T(8,128)(2,1)S(1)}, u32[]{:S(2)}, u32[]{:S(2)}) collective-permute-start(bf16[8,8,768]{2,1,0:T(8,128)(2,1)S(1)} %slice.20), channel_id=1, source_target_pairs={{0,7},{1,0},{2,1},{3,2},{4,3},{5,4},{6,5},{7,6},{8,15},{9,8},{10,9... | collective-permute-start | bytes 294920 | tf_op jit(solution)/shard_map/ppermute | solution.py:23
  27.8 5.1 %collective-permute-start.2 = (bf16[8,8,768]{2,1,0:T(8,128)(2,1)S(1)}, bf16[8,8,768]{2,1,0:T(8,128)(2,1)S(1)}, u32[]{:S(2)}, u32[]{:S(2)}) collective-permute-start(bf16[8,8,768]{2,1,0:T(8,128)(2,1)S(1)} %collective-permute-done), channel_id=1, source_target_pairs={{0,1},{1,2},{2,3},{3,4},{4,5},{5,6},{6,7},{7,0},{8,9},{9,10},{10,1... | collective-permute-start | bytes 294920 | tf_op jit(solution)/shard_map/ppermute | solution.py:23
  43.2 8.1 %collective-permute-start.8 = (bf16[4,8,8,768]{3,2,1,0:T(8,128)(2,1)S(1)}, bf16[4,8,8,768]{3,2,1,0:T(8,128)(2,1)S(1)}, u32[]{:S(2)}, u32[]{:S(2)}) collective-permute-start(bf16[4,8,8,768]{3,2,1,0:T(8,128)(2,1)S(1)} %bitcast.29), channel_id=1, source_target_pairs={{0,8},{8,16},{16,24},{24,0},{1,9},{9,17},{17,25},{25,1},{2,10},{10... | collective-permute-start | bytes 1179656 | tf_op jit(solution)/shard_map/ppermute | solution.py:23
  44.5 6.8 %collective-permute-start.11 = (bf16[4,8,8,768]{3,2,1,0:T(8,128)(2,1)S(1)}, bf16[4,8,8,768]{3,2,1,0:T(8,128)(2,1)S(1)}, u32[]{:S(2)}, u32[]{:S(2)}) collective-permute-start(bf16[4,8,8,768]{3,2,1,0:T(8,128)(2,1)S(1)} %bitcast.32), channel_id=1, source_target_pairs={{0,24},{8,0},{16,8},{24,16},{1,25},{9,1},{17,9},{25,17},{2,26},{10... | collective-permute-start | bytes 1179656 | tf_op jit(solution)/shard_map/ppermute | solution.py:23
  46.3 12.4 %collective-permute-start.10 = (bf16[4,8,8,768]{3,2,1,0:T(8,128)(2,1)S(1)}, bf16[4,8,8,768]{3,2,1,0:T(8,128)(2,1)S(1)}, u32[]{:S(2)}, u32[]{:S(2)}) collective-permute-start(bf16[4,8,8,768]{3,2,1,0:T(8,128)(2,1)S(1)} %bitcast.30), channel_id=1, source_target_pairs={{0,24},{8,0},{16,8},{24,16},{1,25},{9,1},{17,9},{25,17},{2,26},{10... | collective-permute-start | bytes 1179656 | tf_op jit(solution)/shard_map/ppermute | solution.py:23
  47.7 11.9 %collective-permute-start.9 = (bf16[4,8,8,768]{3,2,1,0:T(8,128)(2,1)S(1)}, bf16[4,8,8,768]{3,2,1,0:T(8,128)(2,1)S(1)}, u32[]{:S(2)}, u32[]{:S(2)}) collective-permute-start(bf16[4,8,8,768]{3,2,1,0:T(8,128)(2,1)S(1)} %bitcast.33), channel_id=1, source_target_pairs={{0,8},{8,16},{16,24},{24,0},{1,9},{9,17},{17,25},{25,1},{2,10},{10... | collective-permute-start | bytes 1179656 | tf_op jit(solution)/shard_map/ppermute | solution.py:23
  51.2 16.9 %collective-permute-start.12 = (bf16[4,8,8,768]{3,2,1,0:T(8,128)(2,1)S(1)}, bf16[4,8,8,768]{3,2,1,0:T(8,128)(2,1)S(1)}, u32[]{:S(2)}, u32[]{:S(2)}) collective-permute-start(bf16[4,8,8,768]{3,2,1,0:T(8,128)(2,1)S(1)} %collective-permute-done.8.refs_2_), channel_id=1, source_target_pairs={{0,8},{8,16},{16,24},{24,0},{1,9},{9,17},{17,25},{25,1},{2,10},{10... | collective-permute-start | bytes 1179656 | tf_op jit(solution)/shard_map/ppermute | solution.py:23
  51.3 16.9 %collective-permute-start.13 = (bf16[4,8,8,768]{3,2,1,0:T(8,128)(2,1)S(1)}, bf16[4,8,8,768]{3,2,1,0:T(8,128)(2,1)}, u32[]{:S(2)}, u32[]{:S(2)}) collective-permute-start(bf16[4,8,8,768]{3,2,1,0:T(8,128)(2,1)S(1)} %collective-permute-done.11.refs_5_), channel_id=1, source_target_pairs={{0,24},{8,0},{16,8},{24,16},{1,25},{9,1},{17,9},{25,17},{2,26},{10... | collective-permute-start | bytes 1179656 | tf_op jit(solution)/shard_map/ppermute | solution.py:23
  72.8 17.9 %collective-permute-start.14 = (bf16[768,256]{1,0:T(8,128)(2,1)}, bf16[768,256]{1,0:T(8,128)(2,1)S(1)}, u32[]{:S(2)}, u32[]{:S(2)}) collective-permute-start(bf16[768,256]{1,0:T(8,128)(2,1)} %get-tuple-element.34.refs_0_), channel_id=1, source_target_pairs={{0,1},{1,2},{2,3},{3,4},{4,5},{5,6},{6,7},{7,0},{8,9},{9,10},{10,1... | collective-permute-start | bytes 1179656 | tf_op jit(solution)/shard_map/ppermute | solution.py:23
  72.9 17.8 %collective-permute-start.16 = (bf16[768,256]{1,0:T(8,128)(2,1)}, bf16[768,256]{1,0:T(8,128)(2,1)S(1)}, u32[]{:S(2)}, u32[]{:S(2)}) collective-permute-start(bf16[768,256]{1,0:T(8,128)(2,1)} %get-tuple-element.34.refs_0_), channel_id=1, source_target_pairs={{0,7},{1,0},{2,1},{3,2},{4,3},{5,4},{6,5},{7,6},{8,15},{9,8},{10,9... | collective-permute-start | bytes 1179656 | tf_op jit(solution)/shard_map/ppermute | solution.py:23
  75.6 17.8 %all-to-all-start.1 = ((bf16[4,384,256]{2,1,0:T(8,128)(2,1)}), bf16[4,384,256]{2,1,0:T(8,128)(2,1)S(1)}, u32[]{:S(2)}, u32[]{:S(2)}) async-start(bf16[4,384,256]{2,1,0:T(8,128)(2,1)} %get-tuple-element.33), calls=%async_computation.1 | async-start | bytes 1572864 | tf_op jit(solution)/shard_map/all_to_all | solution.py:410
  79.1 50.3 %all-gather.6.cloned.1.call-start = ((), (), s32[]{:S(2)}) async-start(), calls=%async_computation.3 | async-start | bytes 1310720 | tf_op jit(solution)/shard_map/all_gather | solution.py:417
  90.8 9.2 %collective-permute-start.15 = (bf16[768,256]{1,0:T(8,128)(2,1)S(1)}, bf16[768,256]{1,0:T(8,128)(2,1)}, u32[]{:S(2)}, u32[]{:S(2)}) collective-permute-start(bf16[768,256]{1,0:T(8,128)(2,1)S(1)} %collective-permute-done.14.refs_1_), channel_id=1, source_target_pairs={{0,1},{1,2},{2,3},{3,4},{4,5},{5,6},{6,7},{7,0},{8,9},{9,10},{10,1... | collective-permute-start | bytes 1179656 | tf_op jit(solution)/shard_map/ppermute | solution.py:23
  90.8 9.2 %collective-permute-start.17 = (bf16[768,256]{1,0:T(8,128)(2,1)S(1)}, bf16[768,256]{1,0:T(8,128)(2,1)}, u32[]{:S(2)}, u32[]{:S(2)}) collective-permute-start(bf16[768,256]{1,0:T(8,128)(2,1)S(1)} %collective-permute-done.16.refs_2_), channel_id=1, source_target_pairs={{0,7},{1,0},{2,1},{3,2},{4,3},{5,4},{6,5},{7,6},{8,15},{9,8},{10,9... | collective-permute-start | bytes 1179656 | tf_op jit(solution)/shard_map/ppermute | solution.py:23
  101.7 9.1 %collective-permute-start.18 = (bf16[768,256]{1,0:T(8,128)(2,1)}, bf16[768,256]{1,0:T(8,128)(2,1)S(1)}, u32[]{:S(2)}, u32[]{:S(2)}) collective-permute-start(bf16[768,256]{1,0:T(8,128)(2,1)} %collective-permute-done.15.refs_0_), channel_id=1, source_target_pairs={{0,1},{1,2},{2,3},{3,4},{4,5},{5,6},{6,7},{7,0},{8,9},{9,10},{10,1... | collective-permute-start | bytes 1179656 | tf_op jit(solution)/shard_map/ppermute | solution.py:23
  101.8 9.0 %collective-permute-start.19 = (bf16[768,256]{1,0:T(8,128)(2,1)}, bf16[768,256]{1,0:T(8,128)(2,1)S(1)}, u32[]{:S(2)}, u32[]{:S(2)}) collective-permute-start(bf16[768,256]{1,0:T(8,128)(2,1)} %collective-permute-done.17.refs_1_), channel_id=1, source_target_pairs={{0,7},{1,0},{2,1},{3,2},{4,3},{5,4},{6,5},{7,6},{8,15},{9,8},{10,9... | collective-permute-start | bytes 1179656 | tf_op jit(solution)/shard_map/ppermute | solution.py:23
  110.8 9.4 %collective-permute-start.20 = (bf16[768,256]{1,0:T(8,128)(2,1)S(1)}, bf16[768,256]{1,0:T(8,128)(2,1)}, u32[]{:S(2)}, u32[]{:S(2)}) collective-permute-start(bf16[768,256]{1,0:T(8,128)(2,1)S(1)} %collective-permute-done.18.refs_0_), channel_id=1, source_target_pairs={{0,1},{1,2},{2,3},{3,4},{4,5},{5,6},{6,7},{7,0},{8,9},{9,10},{10,1... | collective-permute-start | bytes 1179656 | tf_op jit(solution)/shard_map/ppermute | solution.py:23
  133.2 5.2 %collective-permute-start.21 = (bf16[272,384]{1,0:T(8,128)(2,1)S(1)}, bf16[272,384]{1,0:T(8,128)(2,1)S(1)}, u32[]{:S(2)}, u32[]{:S(2)}) collective-permute-start(bf16[272,384]{1,0:T(8,128)(2,1)S(1)} %get-tuple-element.59), channel_id=1, source_target_pairs={{0,24},{8,0},{16,8},{24,16},{1,25},{9,1},{17,9},{25,17},{2,26},{10... | collective-permute-start | bytes 626696 | tf_op jit(solution)/shard_map/ppermute | solution.py:23
  133.3 7.6 %collective-permute-start.22 = (bf16[272,384]{1,0:T(8,128)(2,1)S(1)}, bf16[272,384]{1,0:T(8,128)(2,1)S(1)}, u32[]{:S(2)}, u32[]{:S(2)}) collective-permute-start(bf16[272,384]{1,0:T(8,128)(2,1)S(1)} %get-tuple-element.58), channel_id=1, source_target_pairs={{0,8},{8,16},{16,24},{24,0},{1,9},{9,17},{17,25},{25,1},{2,10},{10... | collective-permute-start | bytes 626696 | tf_op jit(solution)/shard_map/ppermute | solution.py:23
  134.7 8.6 %collective-permute-start.23 = (bf16[272,384]{1,0:T(8,128)(2,1)S(1)}, bf16[272,384]{1,0:T(8,128)(2,1)S(1)}, u32[]{:S(2)}, u32[]{:S(2)}) collective-permute-start(bf16[272,384]{1,0:T(8,128)(2,1)S(1)} %get-tuple-element.57), channel_id=1, source_target_pairs={{0,16},{8,24},{16,0},{24,8},{1,17},{9,25},{17,1},{25,9},{2,18},{10... | collective-permute-start | bytes 626696 | tf_op jit(solution)/shard_map/ppermute | solution.py:23
  155.9 6.7 %collective-permute-start.24 = (bf16[4,384,256]{2,1,0:T(8,128)(2,1)S(1)}, bf16[4,384,256]{2,1,0:T(8,128)(2,1)S(1)}, u32[]{:S(2)}, u32[]{:S(2)}) collective-permute-start(bf16[4,384,256]{2,1,0:T(8,128)(2,1)S(1)} %all_to_all.16.mine), channel_id=1, source_target_pairs={{0,32},{32,0},{1,33},{33,1},{2,34},{34,2},{3,35},{35,3},{4,36},{36... | collective-permute-start | bytes 2359304 | tf_op jit(solution)/shard_map/ppermute | solution.py:428
  (20 other events, 336.8 us)
Sparse Core Ops, SparseCore 0:
  9.2 31.0 all-gather.7
  43.0 47.2 all-gather.9
  101.8 27.6 all-gather.5
